TPU v7x, 32 devices: a whole 2x2x4 slice. The times are simulated.
32 devices in a mesh: member: 8 (over z, x), domain: 4 (over y, core).
Axes of the slice: x: 2, y: 2, z: 4, core: 2. Of those that a mesh axis runs over, the one named last changes fastest.
Arguments:
- starting_tracer_fields: float32 [8, 2, 8, 64, 640], P('member', None, None, 'domain'), may hold values from -6 to 6
- surface_exchange_inputs: float32 [8, 2, 64, 640], P('member', None, 'domain'), may hold values from -4 to 4
- diffusivity: float32 [2, 8], replicated, may hold values from 0.04 to 0.2
- mixing: float32 [2, 7], replicated, may hold values from 0.02 to 0.1
- land_mask: int32 [64, 640], replicated, may hold values 0 or 1
- obs_index: int32 [4, 8, 256], P('domain'), may hold values from 0 to 1279
- obs_count: int32 [4, 8], P('domain'), may hold values from 1 to 256, as said below
- obs_value: float32 [4, 8, 256], P('domain'), may hold values from -8 to 8
- obs_error: float32 [4, 8, 256], P('domain'), may hold values from 1 to 16
Outputs:
- analysis: float32 [8, 2, 8, 64, 640], P('member', None, None, 'domain')
Inputs may be any that keep to these rules, and one draw needn't show every extreme that they name: `obs_index`: A cell of the tile's 2 x 640 surface cells, counted row by row. `obs_count`: slots below the count hold observations, the rest are unused; in every domain the last tile holds exactly 256.
All inputs are finite; a program needn't handle non-finite values.
Results may differ from a plain program's by a relative error of at most 0.0001.
Values sent between devices are 32-bit elements; how exact they have to be, the bound alone decides.
A program may use at most 64 MiB of HBM per device.

v0:
```python
import jax
import jax.numpy as jnp
from jax import lax
from jax.sharding import PartitionSpec as P

STEPS = 2


def with_halo(shard, sides, width):
    for axis, dim in sides:
        size, length = (lax.axis_size(axis), shard.shape[dim])
        up = [(i, (i + 1) % size) for i in range(size - 1)]
        down = [(j, i) for i, j in up]
        last = lax.slice_in_dim(shard, length - width, length, axis=dim)
        initial = lax.slice_in_dim(shard, 0, width, axis=dim)
        before = lax.ppermute(last, axis, up)
        after = lax.ppermute(initial, axis, down)
        shard = jnp.concatenate([before, shard, after], axis=dim)
    return shard


def stencil(padded, mask_rows, diffusivity, mixing, surface_exchange_inputs):
    middle = padded[:, :, 1:-1]
    mask_mid = mask_rows[1:-1]
    upper_row = padded[:, :, 2:]
    lower_row = padded[:, :, :-2]
    east_cell = jnp.roll(middle, -1, axis=3)
    west_cell = jnp.roll(middle, 1, axis=3)
    lateral = mask_rows[2:] * (upper_row - middle) + mask_rows[:-2] * (lower_row - middle)
    lateral = lateral + jnp.roll(mask_mid, -1, axis=1) * (east_cell - middle)
    lateral = lateral + jnp.roll(mask_mid, 1, axis=1) * (west_cell - middle)
    downward_flux = mixing[:, :, None, None] * (middle[:, 1:] - middle[:, :-1])
    empty_level = jnp.zeros_like(middle[:, :1])
    vertical = jnp.concatenate([downward_flux, empty_level], axis=1) - jnp.concatenate(
        [empty_level, downward_flux], axis=1
    )
    tendency = diffusivity[:, :, None, None] * lateral + vertical
    tendency = tendency.at[:, 0].add(surface_exchange_inputs)
    return middle + mask_mid * tendency


def partial_sums(observed, values, errors, active):
    average = jnp.mean(observed, axis=0)
    anomaly = observed - average[None, :]
    weight_obs = active / errors
    gram = jnp.dot(anomaly * weight_obs[None, :], anomaly.T, precision=lax.Precision.HIGHEST)
    pull = jnp.dot(anomaly, weight_obs * (values - average), precision=lax.Precision.HIGHEST)
    return (gram, pull)


def transform(gram, pull):
    count = gram.shape[0]
    identity = jnp.eye(count, dtype=gram.dtype)
    factor = jnp.linalg.cholesky(gram + (count - 1.0) * identity)
    inverse = jax.scipy.linalg.solve_triangular(factor, identity, lower=True)
    mean_weight = jnp.dot(
        inverse.T,
        jnp.dot(inverse, pull, precision=lax.Precision.HIGHEST),
        precision=lax.Precision.HIGHEST,
    )
    weights = mean_weight[:, None] + jnp.sqrt(count - 1.0) * inverse.T
    return weights - jnp.mean(weights, axis=0, keepdims=True) + 1.0 / count


def update(kernel, tile_block, tile_mask):
    count = tile_block.shape[0]
    updated = jnp.einsum(
        "jm,jn->mn", kernel, tile_block.reshape(count, -1), precision=lax.Precision.HIGHEST
    )
    return jnp.where(tile_mask > 0, updated.reshape(tile_block.shape), tile_block)


def shards(
    starting_tracer_fields,
    surface_exchange_inputs,
    diffusivity,
    mixing,
    land_mask,
    obs_index,
    obs_count,
    obs_value,
    obs_error,
):
    ocean_state = starting_tracer_fields[0]
    row_count = ocean_state.shape[2]
    longitudes = ocean_state.shape[3]
    subregion_offset = lax.axis_index("domain")
    sea_mask = land_mask.astype(jnp.float32)
    padded_mask = jnp.pad(sea_mask, ((1, 1), (0, 0)))
    local_mask = lax.dynamic_slice_in_dim(
        padded_mask, subregion_offset * row_count, row_count + 2, 0
    )
    for _ in range(STEPS):
        padded = with_halo(ocean_state, (("domain", 2),), 1)
        ocean_state = stencil(padded, local_mask, diffusivity, mixing, surface_exchange_inputs[0])
    stacked = ocean_state.reshape(1, -1, row_count, longitudes)
    members = lax.axis_size("member")
    tile_rows = row_count // members
    tile_index = lax.axis_index("member")
    tile_mask = lax.dynamic_slice_in_dim(local_mask[1:-1], tile_index * tile_rows, tile_rows, 0)
    slot_rank = jnp.arange(obs_index.shape[2], dtype=jnp.int32)
    tile_block = lax.all_to_all(stacked, "member", split_axis=2, concat_axis=0, tiled=True)
    surface = tile_block[:, 0].reshape(members, -1)
    obs_slots = lax.dynamic_index_in_dim(obs_index[0], tile_index, 0, keepdims=False)
    observed = surface[:, obs_slots]
    limit = lax.dynamic_index_in_dim(obs_count[0], tile_index, 0, keepdims=False)
    active = (slot_rank < limit).astype(jnp.float32)
    values = lax.dynamic_index_in_dim(obs_value[0], tile_index, 0, keepdims=False)
    errors = lax.dynamic_index_in_dim(obs_error[0], tile_index, 0, keepdims=False)
    gram, pull = partial_sums(observed, values, errors, active)
    gram, pull = lax.psum((gram, pull), "member")
    kernel = transform(gram, pull)
    updated = update(kernel, tile_block, tile_mask)
    returned = lax.all_to_all(updated, "member", split_axis=0, concat_axis=2, tiled=True)
    return returned.reshape(starting_tracer_fields.shape)


def solution(mesh):
    placed = (
        P("member", None, None, "domain", None),
        P("member", None, "domain", None),
        P(),
        P(),
        P(),
        P("domain", None, None),
        P("domain", None),
        P("domain", None, None),
        P("domain", None, None),
    )
    return jax.shard_map(
        shards,
        mesh=mesh,
        in_specs=placed,
        out_specs=P("member", None, None, "domain", None),
        check_vma=False,
    )
```

profile of v0, /device:TPU:0, one launch (start us, length us, event | category | flops | bytes accessed | tf_op | source)
XLA Modules:
  0.0 90.1 jit_solution(5743181250172521186)
XLA Ops:
  0.0 0.0 copy-start
  0.0 0.0 copy-start.1
  0.0 1.2 %fusion.61 = (f32[2,8,1,640]{3,2,1,0:T(1,128)S(1)}, f32[2,8,1,640]{3,2,1,0:T(1,128)S(1)}) fusion(f32[2,8,16,640]{3,2,1,0:T(8,128)} %bitcast.78), kind=kLoop, calls=%fused_computation.108 | loop fusion | bytes 163840 | tf_op jit(solution)/shard_map/slice | solution.py:15
  1.2 1.3 %collective-permute-start = (f32[2,8,1,640]{3,2,1,0:T(1,128)S(1)}, f32[2,8,1,640]{3,2,1,0:T(1,128)S(1)}, u32[]{:S(2)}, u32[]{:S(2)}) collective-permute-start(f32[2,8,1,640]{3,2,1,0:T(1,128)S(1)} %get-tuple-element.43), channel_id=1, source_target_pairs={{1,0},{2,1},{3,2},{5,4},{6,5},{7,6},{9,8},{10,9},{11,10},{13,12},{... | collective-permute-start | bytes 122888 | tf_op jit(solution)/shard_map/ppermute | solution.py:17
  2.5 3.0 %collective-permute-start.1 = (f32[2,8,1,640]{3,2,1,0:T(1,128)S(1)}, f32[2,8,1,640]{3,2,1,0:T(1,128)S(1)}, u32[]{:S(2)}, u32[]{:S(2)}) collective-permute-start(f32[2,8,1,640]{3,2,1,0:T(1,128)S(1)} %get-tuple-element.44), channel_id=1, source_target_pairs={{0,1},{1,2},{2,3},{4,5},{5,6},{6,7},{8,9},{9,10},{10,11},{12,13},{... | collective-permute-start | bytes 122888 | tf_op jit(solution)/shard_map/ppermute | solution.py:16
  5.5 1.1 %fusion.59 = (f32[2,8,16,1]{3,2,1,0:T(8,128)S(1)}, f32[2,8,16,1]{3,2,1,0:T(8,128)S(1)}) fusion(f32[2,8,16,640]{3,2,1,0:T(8,128)} %bitcast.79), kind=kLoop, calls=%fused_computation.106 | loop fusion | bytes 4096 | tf_op jit(solution)/shard_map/jit(_roll_static)/slice | solution.py:28
  6.6 0.0 copy-done.1
  6.6 0.0 copy-start.3
  6.6 0.2 fusion.60
  6.9 0.7 copy-done.3
  7.6 0.1 pad_dynamic-slice_fusion.1
  7.7 0.1 pad_dynamic-slice_fusion.2
  7.7 0.0 copy-start.4
  7.8 0.6 copy-done.4
  8.4 0.1 fusion.25
  8.5 0.1 pad_maximum_fusion.4
  8.6 0.0 collective-permute-done
  8.6 0.0 collective-permute-done.1
  8.6 0.0 copy-start.5
  8.7 0.7 copy-done.5
  9.3 0.6 fusion.15
  9.9 0.3 copy-done.2
  10.2 0.1 multiply_add_fusion.1
  10.3 0.1 fusion.58
  10.4 0.1 fusion.24
  10.5 0.2 fusion.57
  10.8 1.3 %collective-permute-start.2 = (f32[2,8,1,640]{3,2,1,0:T(1,128)S(1)}, f32[2,8,1,640]{3,2,1,0:T(1,128)S(1)}, u32[]{:S(2)}, u32[]{:S(2)}) collective-permute-start(f32[2,8,1,640]{3,2,1,0:T(1,128)S(1)} %get-tuple-element.37), channel_id=1, source_target_pairs={{1,0},{2,1},{3,2},{5,4},{6,5},{7,6},{9,8},{10,9},{11,10},{13,12},{... | collective-permute-start | bytes 122888 | tf_op jit(solution)/shard_map/ppermute | solution.py:17
  12.1 5.1 %collective-permute-start.3 = (f32[2,8,1,640]{3,2,1,0:T(1,128)S(1)}, f32[2,8,1,640]{3,2,1,0:T(1,128)S(1)}, u32[]{:S(2)}, u32[]{:S(2)}) collective-permute-start(f32[2,8,1,640]{3,2,1,0:T(1,128)S(1)} %get-tuple-element.38), channel_id=1, source_target_pairs={{0,1},{1,2},{2,3},{4,5},{5,6},{6,7},{8,9},{9,10},{10,11},{12,13},{... | collective-permute-start | bytes 122888 | tf_op jit(solution)/shard_map/ppermute | solution.py:16
  17.2 0.1 fusion.56
  17.3 0.0 collective-permute-done.2
  17.3 0.7 collective-permute-done.3
  18.1 0.6 fusion.6
  18.7 0.1 multiply_add_fusion
  18.8 1.0 %copy.32 = f32[1,16,16,640]{3,1,0,2:T(8,128)} copy(f32[1,16,16,640]{3,2,1,0:T(8,128)S(1)} %bitcast.85) | data formatting | bytes 1310720 | tf_op jit(solution)/shard_map/reshape | solution.py:96
  19.8 5.8 %all-to-all-start = ((f32[1,16,16,640]{3,1,0,2:T(8,128)}), f32[1,16,16,640]{3,1,0,2:T(8,128)S(1)}, u32[]{:S(2)}, u32[]{:S(2)}) async-start(f32[1,16,16,640]{3,1,0,2:T(8,128)} %copy.32), calls=%async_computation | async-start | bytes 1310720 | tf_op jit(solution)/shard_map/all_to_all | solution.py:102
  25.6 0.0 copy-done
  25.6 0.6 constant_dynamic-slice_fusion.2
  26.2 0.7 compare_select_fusion
  26.9 0.7 constant_dynamic-slice_fusion
  27.7 15.9 %all-to-all-done = f32[1,16,16,640]{3,1,0,2:T(8,128)S(1)} async-done(((f32[1,16,16,640]{3,1,0,2:T(8,128)}), f32[1,16,16,640]{3,1,0,2:T(8,128)S(1)}, u32[]{:S(2)}, u32[]{:S(2)}) %all-to-all-start) | async-done | bytes 655392 | tf_op jit(solution)/shard_map/all_to_all | solution.py:102
  43.6 0.4 copy.55
  44.0 0.2 copy.34
  44.2 0.7 gather_fusion
  45.0 0.1 reduce_sum.18
  45.1 0.6 subtract_multiply_fusion
  45.7 0.2 convolution_bitcast_fusion.2
  46.0 0.5 fusion.27
  46.5 20.4 %all-reduce.5 = (f32[8,8]{0,1:T(8,128)S(1)}, f32[8]{0:T(128)S(1)}) all-reduce(f32[8,8]{0,1:T(8,128)S(1)} %fusion.27, f32[8]{0:T(128)S(1)} %convolution_bitcast_fusion.2), channel_id=1, replica_groups=mesh['member'=8,'domain'=4] {'member'}, use_global_device_ids=true, to_apply=%region_1.2 | all-reduce | flops 72 | bytes 576 | tf_op jit(solution)/shard_map/psum | solution.py:111
  66.9 0.1 copy.36
  67.0 0.7 cholesky.17
  67.7 0.1 copy.37
  67.8 0.1 select_reduce_fusion
  67.9 0.6 compare_reduce_fusion
  68.6 0.6 select_select_fusion
  69.2 0.1 copy.39
  69.3 0.6 custom-call.7
  69.9 0.1 fusion.36
  70.0 0.1 convolution_bitcast_fusion.1
  70.2 0.1 convolution_bitcast_fusion
  70.3 0.1 fusion.45
  70.4 1.4 %convolution_select_fusion = f32[8,16,2,640]{3,0,2,1:T(8,128)S(1)} fusion(f32[1,16,8,2,640]{4,1,3,2,0:T(8,128)S(1)} %bitcast.84, pred[2,640]{1,0:T(4,128)(4,1)S(1)} %fusion.35, f32[8,8]{0,1:T(8,128)S(1)} %fusion.36, f32[8]{0:T(128)S(1)} %broadcast_multiply_fusion.1, f32[8]{0:T(128)S(1)} %convolution_bitcast_fusion), kind=kOutput, calls=%fused_computation.1 | convolution fusion | flops 15892736 | bytes 1312320 | tf_op jit(solution)/shard_map/jm,jn->mn/dot_general | solution.py:67
  71.8 0.3 copy.42
  72.2 16.9 %all_to_all.33 = f32[8,16,2,640]{3,2,1,0:T(2,128)S(1)} all-to-all(f32[8,16,2,640]{3,2,1,0:T(2,128)S(1)} %copy.42), channel_id=1, replica_groups=mesh['member'=8,'domain'=4] {'member'}, dimensions={0} | all-to-all | bytes 1310720 | tf_op jit(solution)/shard_map/all_to_all | solution.py:114
  89.1 1.0 %copy.44 = f32[1,2,8,16,640]{4,3,2,1,0:T(8,128)} copy(f32[1,2,8,16,640]{4,2,1,3,0:T(8,128)S(1)} %bitcast.86) | data formatting | bytes 1310720 | tf_op jit(solution)/shard_map/reshape | solution.py:115
  (12 shorter events, 0.2 us)
Async XLA Ops:
  0.0 25.6 %copy-start = (s32[1,8]{1,0:T(1,128)S(1)}, s32[1,8]{1,0:T(1,128)}, u32[]{:S(2)}) copy-start(s32[1,8]{1,0:T(1,128)} %param.19) | copy-start | bytes 100
  0.0 6.6 %copy-start.1 = (f32[1,2,8,16,640]{4,3,2,1,0:T(8,128)S(1)}, f32[1,2,8,16,640]{4,3,2,1,0:T(8,128)}, u32[]{:S(2)}) copy-start(f32[1,2,8,16,640]{4,3,2,1,0:T(8,128)} %param.13) | copy-start | bytes 1966084
  1.2 7.4 %collective-permute-start = (f32[2,8,1,640]{3,2,1,0:T(1,128)S(1)}, f32[2,8,1,640]{3,2,1,0:T(1,128)S(1)}, u32[]{:S(2)}, u32[]{:S(2)}) collective-permute-start(f32[2,8,1,640]{3,2,1,0:T(1,128)S(1)} %get-tuple-element.43), channel_id=1, source_target_pairs={{1,0},{2,1},{3,2},{5,4},{6,5},{7,6},{9,8},{10,9},{11,10},{13,12},{... | collective-permute-start | bytes 122888 | tf_op jit(solution)/shard_map/ppermute | solution.py:17
  2.5 6.1 %collective-permute-start.1 = (f32[2,8,1,640]{3,2,1,0:T(1,128)S(1)}, f32[2,8,1,640]{3,2,1,0:T(1,128)S(1)}, u32[]{:S(2)}, u32[]{:S(2)}) collective-permute-start(f32[2,8,1,640]{3,2,1,0:T(1,128)S(1)} %get-tuple-element.44), channel_id=1, source_target_pairs={{0,1},{1,2},{2,3},{4,5},{5,6},{6,7},{8,9},{9,10},{10,11},{12,13},{... | collective-permute-start | bytes 122888 | tf_op jit(solution)/shard_map/ppermute | solution.py:16
  6.6 0.9 %copy-start.3 = (s32[64,640]{1,0:T(8,128)S(1)}, s32[64,640]{1,0:T(8,128)}, u32[]{:S(2)}) copy-start(s32[64,640]{1,0:T(8,128)} %param.17) | copy-start | bytes 491524
  7.7 0.7 copy-start.4
  8.6 0.7 copy-start.5
  9.3 0.9 copy-start.2
  10.8 6.6 %collective-permute-start.2 = (f32[2,8,1,640]{3,2,1,0:T(1,128)S(1)}, f32[2,8,1,640]{3,2,1,0:T(1,128)S(1)}, u32[]{:S(2)}, u32[]{:S(2)}) collective-permute-start(f32[2,8,1,640]{3,2,1,0:T(1,128)S(1)} %get-tuple-element.37), channel_id=1, source_target_pairs={{1,0},{2,1},{3,2},{5,4},{6,5},{7,6},{9,8},{10,9},{11,10},{13,12},{... | collective-permute-start | bytes 122888 | tf_op jit(solution)/shard_map/ppermute | solution.py:17
  12.1 6.0 %collective-permute-start.3 = (f32[2,8,1,640]{3,2,1,0:T(1,128)S(1)}, f32[2,8,1,640]{3,2,1,0:T(1,128)S(1)}, u32[]{:S(2)}, u32[]{:S(2)}) collective-permute-start(f32[2,8,1,640]{3,2,1,0:T(1,128)S(1)} %get-tuple-element.38), channel_id=1, source_target_pairs={{0,1},{1,2},{2,3},{4,5},{5,6},{6,7},{8,9},{9,10},{10,11},{12,13},{... | collective-permute-start | bytes 122888 | tf_op jit(solution)/shard_map/ppermute | solution.py:16
  19.8 23.8 %all-to-all-start = ((f32[1,16,16,640]{3,1,0,2:T(8,128)}), f32[1,16,16,640]{3,1,0,2:T(8,128)S(1)}, u32[]{:S(2)}, u32[]{:S(2)}) async-start(f32[1,16,16,640]{3,1,0,2:T(8,128)} %copy.32), calls=%async_computation | async-start | bytes 1310720 | tf_op jit(solution)/shard_map/all_to_all | solution.py:102
where the time goes:
time: 90.7 us; the launch traced here: 90.1 us
  blocking collectives  37.3 us (41%)
  waiting for transfers between devices  16.7 us (18%)
  starting transfers between devices  16.6 us (18%)
  local copies, waits for them, and re-layouts  10.7 us (12%)
  other arithmetic  6.05 us (7%)
  matrix products  2.55 us (3%)
    psum x1, blocking collectives, shards(): gram, pull = lax.psum((gram, pull), 'member')  20.4 us
    all_to_all x1, blocking collectives, shards(): lax.all_to_all(updated, 'member', split_axis=0, concat_axis=2, tiled=True)  16.9 us
    all_to_all x1, waiting for transfers between devices, shards(): lax.all_to_all(stacked, 'member', split_axis=2, concat_axis=0, tiled=True)  15.9 us
    ppermute x2, starting transfers between devices, with_halo(): before = lax.ppermute(last, axis, up)  8.18 us
    all_to_all x1, starting transfers between devices, shards(): lax.all_to_all(stacked, 'member', split_axis=2, concat_axis=0, tiled=True)  5.81 us
    ppermute x2, starting transfers between devices, with_halo(): after = lax.ppermute(initial, axis, down)  2.58 us
    unnamed x12, local copies, waits for them, and re-layouts  2.27 us
  transfers between devices with their start and end apart: 5, of which 2 were waited for; matrix products, arithmetic and copies ran while one was open for 4% of the time, Pallas kernels for 0%

commit v1 on v0

--- a/solution.py
+++ b/solution.py
@@ -99,7 +99,9 @@
     tile_index = lax.axis_index("member")
     tile_mask = lax.dynamic_slice_in_dim(local_mask[1:-1], tile_index * tile_rows, tile_rows, 0)
     slot_rank = jnp.arange(obs_index.shape[2], dtype=jnp.int32)
-    tile_block = lax.all_to_all(stacked, "member", split_axis=2, concat_axis=0, tiled=True)
+    pieces = jnp.split(stacked, lax.axis_size("member"), axis=2)
+    incoming = lax.all_to_all(jnp.stack(pieces), "member", 0, 0)
+    tile_block = jnp.concatenate(incoming, axis=0)
     surface = tile_block[:, 0].reshape(members, -1)
     obs_slots = lax.dynamic_index_in_dim(obs_index[0], tile_index, 0, keepdims=False)
     observed = surface[:, obs_slots]

time: 90.7 us -> 94 us (1.036)
  local copies, waits for them, and re-layouts: 10.7 us -> 14.3 us
    unnamed x12 -> x22, local copies, waits for them, and re-layouts: 2.27 us -> 7.77 us
    another operation x0 -> x2, local copies, waits for them, and re-layouts: none -> 1.21 us  [the longest x1 0.67 us: shards(): incoming = lax.all_to_all(jnp.stack(pieces), 'member', 0, 0)]
    slice x2, local copies, waits for them, and re-layouts: 1.26 us -> 0.12 us  [with_halo(): initial = lax.slice_in_dim(shard, 0, width, axis=dim)]
    reshape x1 -> x0, local copies, waits for them, and re-layouts: 1.04 us -> none  [shards(): stacked = ocean_state.reshape(1, -1, row_count, longitudes)]
    slice x4, local copies, waits for them, and re-layouts: 1.64 us -> 0.67 us  [stencil(): west_cell = jnp.roll(middle, 1, axis=3)]
  transfers between devices with their start and end apart: 5 -> 5, of which waited for: 2 -> 2; matrix products, arithmetic and copies ran while one was open for 4% -> 3% of each run, Pallas kernels for 0% -> 0%
where the time goes in v1:
time: 94 us; the launch traced here: 93.5 us
  blocking collectives  37.3 us (40%)
  waiting for transfers between devices  16.7 us (18%)
  starting transfers between devices  16.6 us (18%)
  local copies, waits for them, and re-layouts  14.3 us (15%)
  other arithmetic  6.08 us (6%)
  matrix products  2.29 us (2%)
    psum x1, blocking collectives, shards(): gram, pull = lax.psum((gram, pull), 'member')  20.4 us
    all_to_all x1, blocking collectives, shards(): lax.all_to_all(updated, 'member', split_axis=0, concat_axis=2, tiled=True)  16.9 us
    all_to_all x1, waiting for transfers between devices, shards(): incoming = lax.all_to_all(jnp.stack(pieces), 'member', 0, 0)  15.9 us
    ppermute x2, starting transfers between devices, with_halo(): before = lax.ppermute(last, axis, up)  8.18 us
    unnamed x22, local copies, waits for them, and re-layouts  7.77 us
    all_to_all x1, starting transfers between devices, shards(): incoming = lax.all_to_all(jnp.stack(pieces), 'member', 0, 0)  5.81 us
    ppermute x2, starting transfers between devices, with_halo(): after = lax.ppermute(initial, axis, down)  2.58 us
  transfers between devices with their start and end apart: 5, of which 2 were waited for; matrix products, arithmetic and copies ran while one was open for 3% of the time, Pallas kernels for 0%

profile of v1, /device:TPU:0, one launch (start us, length us, event | category | flops | bytes accessed | tf_op | source)
XLA Modules:
  0.0 93.5 jit_solution(16959842292837205797)
XLA Ops:
  0.0 1.1 %copy.61 = f32[1,2,8,16,640]{4,3,1,2,0:T(8,128)S(1)} copy(f32[1,2,8,16,640]{4,3,2,1,0:T(8,128)} %param.13) | data formatting | bytes 1310720 | tf_op args[0]
  1.2 1.3 %collective-permute-start = (f32[2,8,1,640]{3,2,0,1:T(1,128)S(1)}, f32[2,8,1,640]{3,2,0,1:T(1,128)S(1)}, u32[]{:S(2)}, u32[]{:S(2)}) collective-permute-start(f32[2,8,1,640]{3,2,0,1:T(1,128)S(1)} %get-tuple-element.43), channel_id=1, source_target_pairs={{1,0},{2,1},{3,2},{5,4},{6,5},{7,6},{9,8},{10,9},{11,10},{13,12},{... | collective-permute-start | bytes 122888 | tf_op jit(solution)/shard_map/ppermute | solution.py:17
  2.5 3.0 %collective-permute-start.1 = (f32[2,8,1,640]{3,2,0,1:T(1,128)S(1)}, f32[2,8,1,640]{3,2,0,1:T(1,128)S(1)}, u32[]{:S(2)}, u32[]{:S(2)}) collective-permute-start(f32[2,8,1,640]{3,2,0,1:T(1,128)S(1)} %get-tuple-element.44), channel_id=1, source_target_pairs={{0,1},{1,2},{2,3},{4,5},{5,6},{6,7},{8,9},{9,10},{10,11},{12,13},{... | collective-permute-start | bytes 122888 | tf_op jit(solution)/shard_map/ppermute | solution.py:16
  5.6 0.1 fusion.65
  5.7 0.2 fusion.66
  5.9 0.7 copy-done.4
  6.6 0.1 copy.37
  6.7 0.1 pad_dynamic-slice_fusion.1
  6.8 0.1 pad_dynamic-slice_fusion.2
  6.9 0.1 fusion.23
  7.1 0.1 pad_maximum_fusion.4
  7.1 0.6 copy-done.5
  7.7 0.1 copy.36
  7.8 0.6 fusion.15
  8.4 0.3 copy-done.2
  8.7 0.2 copy-done.1
  9.0 0.1 multiply_add_fusion.1
  9.0 0.1 fusion.64
  9.1 0.1 fusion.22
  9.2 0.2 fusion.63
  9.5 1.3 %collective-permute-start.2 = (f32[2,8,1,640]{3,2,0,1:T(1,128)S(1)}, f32[2,8,1,640]{3,2,0,1:T(1,128)S(1)}, u32[]{:S(2)}, u32[]{:S(2)}) collective-permute-start(f32[2,8,1,640]{3,2,0,1:T(1,128)S(1)} %get-tuple-element.37), channel_id=1, source_target_pairs={{1,0},{2,1},{3,2},{5,4},{6,5},{7,6},{9,8},{10,9},{11,10},{13,12},{... | collective-permute-start | bytes 122888 | tf_op jit(solution)/shard_map/ppermute | solution.py:17
  10.8 5.1 %collective-permute-start.3 = (f32[2,8,1,640]{3,2,0,1:T(1,128)S(1)}, f32[2,8,1,640]{3,2,0,1:T(1,128)S(1)}, u32[]{:S(2)}, u32[]{:S(2)}) collective-permute-start(f32[2,8,1,640]{3,2,0,1:T(1,128)S(1)} %get-tuple-element.38), channel_id=1, source_target_pairs={{0,1},{1,2},{2,3},{4,5},{5,6},{6,7},{8,9},{9,10},{10,11},{12,13},{... | collective-permute-start | bytes 122888 | tf_op jit(solution)/shard_map/ppermute | solution.py:16
  15.9 0.1 fusion.62
  16.0 0.7 collective-permute-done.3
  16.8 0.6 fusion.6
  17.4 0.1 multiply_add_fusion
  17.6 0.7 fusion.35
  18.2 0.7 fusion.34
  18.9 0.7 fusion.33
  19.6 0.7 fusion.32
  20.2 0.7 fusion.31
  20.9 0.7 fusion.30
  21.6 0.7 fusion.29
  22.2 0.7 fusion.28
  22.9 5.8 %all-to-all-start = ((f32[8,1,16,2,640]{4,3,2,1,0:T(2,128)}), f32[8,1,16,2,640]{4,3,2,1,0:T(2,128)S(1)}, u32[]{:S(2)}, u32[]{:S(2)}) async-start(f32[8,1,16,2,640]{4,3,2,1,0:T(2,128)} %fusion.28), calls=%async_computation | async-start | bytes 1310720 | tf_op jit(solution)/shard_map/all_to_all | solution.py:103
  28.7 0.6 constant_dynamic-slice_fusion.2
  29.3 0.7 compare_select_fusion
  30.0 0.7 constant_dynamic-slice_fusion
  30.8 15.9 %all-to-all-done = f32[8,1,16,2,640]{4,3,2,1,0:T(2,128)S(1)} async-done(((f32[8,1,16,2,640]{4,3,2,1,0:T(2,128)}), f32[8,1,16,2,640]{4,3,2,1,0:T(2,128)S(1)}, u32[]{:S(2)}, u32[]{:S(2)}) %all-to-all-start) | async-done | bytes 655392 | tf_op jit(solution)/shard_map/all_to_all | solution.py:103
  46.7 0.4 copy.60
  47.1 0.2 copy.40
  47.3 0.7 gather_fusion
  48.1 0.1 reduce_sum.18
  48.2 0.6 subtract_multiply_fusion
  48.8 0.2 convolution_bitcast_fusion.2
  49.1 0.5 fusion.25
  49.6 20.4 %all-reduce.5 = (f32[8,8]{0,1:T(8,128)S(1)}, f32[8]{0:T(128)S(1)}) all-reduce(f32[8,8]{0,1:T(8,128)S(1)} %fusion.25, f32[8]{0:T(128)S(1)} %convolution_bitcast_fusion.2), channel_id=1, replica_groups=mesh['member'=8,'domain'=4] {'member'}, use_global_device_ids=true, to_apply=%region_1.2 | all-reduce | flops 72 | bytes 576 | tf_op jit(solution)/shard_map/psum | solution.py:113
  70.0 0.1 copy.42
  70.1 0.7 cholesky.17
  70.8 0.1 copy.43
  70.9 0.1 select_reduce_fusion
  71.0 0.6 compare_reduce_fusion
  71.7 0.6 select_select_fusion
  72.3 0.1 copy.45
  72.4 0.6 custom-call.7
  73.0 0.1 fusion.42
  73.1 0.1 convolution_bitcast_fusion.1
  73.3 0.1 convolution_bitcast_fusion
  73.4 0.1 fusion.51
  73.5 0.5 reshape_reshape.3
  74.1 1.1 %convolution_select_fusion = f32[8,16,2,640]{3,0,2,1:T(8,128)S(1)} fusion(f32[16,2,640,8]{2,3,1,0:T(8,128)S(1)} %bitcast.119, pred[2,640]{1,0:T(4,128)(4,1)S(1)} %fusion.41, f32[8,8]{0,1:T(8,128)S(1)} %fusion.42, f32[8]{0:T(128)S(1)} %broadcast_multiply_fusion.1, f32[8]{0:T(128)S(1)} %convolution_bitcast_fusion, f32[8,1,16,2,640]{4,3,2,1,0:T(2,128)S(1)} %all-to-all-done), kind=kOutput, calls=%fused_computation.1 | convolution fusion | flops 15892736 | bytes 1967680 | tf_op jit(solution)/shard_map/jm,jn->mn/dot_general | solution.py:67
  75.2 0.3 copy.48
  75.6 16.9 %all_to_all.20 = f32[8,16,2,640]{3,2,1,0:T(2,128)S(1)} all-to-all(f32[8,16,2,640]{3,2,1,0:T(2,128)S(1)} %copy.48), channel_id=1, replica_groups=mesh['member'=8,'domain'=4] {'member'}, dimensions={0} | all-to-all | bytes 1310720 | tf_op jit(solution)/shard_map/all_to_all | solution.py:116
  92.5 1.0 %copy.50 = f32[1,2,8,16,640]{4,3,2,1,0:T(8,128)} copy(f32[1,2,8,16,640]{4,2,1,3,0:T(8,128)S(1)} %bitcast.120) | data formatting | bytes 1310720 | tf_op jit(solution)/shard_map/reshape | solution.py:117
  (24 shorter events, 0.3 us)
Async XLA Ops:
  0.0 28.7 %copy-start = (s32[1,8]{1,0:T(1,128)S(1)}, s32[1,8]{1,0:T(1,128)}, u32[]{:S(2)}) copy-start(s32[1,8]{1,0:T(1,128)} %param.19) | copy-start | bytes 100
  1.2 6.6 %collective-permute-start = (f32[2,8,1,640]{3,2,0,1:T(1,128)S(1)}, f32[2,8,1,640]{3,2,0,1:T(1,128)S(1)}, u32[]{:S(2)}, u32[]{:S(2)}) collective-permute-start(f32[2,8,1,640]{3,2,0,1:T(1,128)S(1)} %get-tuple-element.43), channel_id=1, source_target_pairs={{1,0},{2,1},{3,2},{5,4},{6,5},{7,6},{9,8},{10,9},{11,10},{13,12},{... | collective-permute-start | bytes 122888 | tf_op jit(solution)/shard_map/ppermute | solution.py:17
  2.5 5.3 %collective-permute-start.1 = (f32[2,8,1,640]{3,2,0,1:T(1,128)S(1)}, f32[2,8,1,640]{3,2,0,1:T(1,128)S(1)}, u32[]{:S(2)}, u32[]{:S(2)}) collective-permute-start(f32[2,8,1,640]{3,2,0,1:T(1,128)S(1)} %get-tuple-element.44), channel_id=1, source_target_pairs={{0,1},{1,2},{2,3},{4,5},{5,6},{6,7},{8,9},{9,10},{10,11},{12,13},{... | collective-permute-start | bytes 122888 | tf_op jit(solution)/shard_map/ppermute | solution.py:16
  5.7 1.0 %copy-start.3 = (s32[64,640]{1,0:T(8,128)S(1)}, s32[64,640]{1,0:T(8,128)}, u32[]{:S(2)}) copy-start(s32[64,640]{1,0:T(8,128)} %param.17) | copy-start | bytes 491524
  5.9 0.7 copy-start.4
  7.1 0.7 copy-start.5
  7.8 0.9 copy-start.2
  7.8 1.1 %copy-start.1 = (f32[1,2,8,16,640]{4,3,2,1,0:T(8,128)S(1)}, f32[1,2,8,16,640]{4,3,2,1,0:T(8,128)}, u32[]{:S(2)}) copy-start(f32[1,2,8,16,640]{4,3,2,1,0:T(8,128)} %param.13) | copy-start | bytes 1966084
  9.5 6.6 %collective-permute-start.2 = (f32[2,8,1,640]{3,2,0,1:T(1,128)S(1)}, f32[2,8,1,640]{3,2,0,1:T(1,128)S(1)}, u32[]{:S(2)}, u32[]{:S(2)}) collective-permute-start(f32[2,8,1,640]{3,2,0,1:T(1,128)S(1)} %get-tuple-element.37), channel_id=1, source_target_pairs={{1,0},{2,1},{3,2},{5,4},{6,5},{7,6},{9,8},{10,9},{11,10},{13,12},{... | collective-permute-start | bytes 122888 | tf_op jit(solution)/shard_map/ppermute | solution.py:17
  10.8 6.0 %collective-permute-start.3 = (f32[2,8,1,640]{3,2,0,1:T(1,128)S(1)}, f32[2,8,1,640]{3,2,0,1:T(1,128)S(1)}, u32[]{:S(2)}, u32[]{:S(2)}) collective-permute-start(f32[2,8,1,640]{3,2,0,1:T(1,128)S(1)} %get-tuple-element.38), channel_id=1, source_target_pairs={{0,1},{1,2},{2,3},{4,5},{5,6},{6,7},{8,9},{9,10},{10,11},{12,13},{... | collective-permute-start | bytes 122888 | tf_op jit(solution)/shard_map/ppermute | solution.py:16
  22.9 23.8 %all-to-all-start = ((f32[8,1,16,2,640]{4,3,2,1,0:T(2,128)}), f32[8,1,16,2,640]{4,3,2,1,0:T(2,128)S(1)}, u32[]{:S(2)}, u32[]{:S(2)}) async-start(f32[8,1,16,2,640]{4,3,2,1,0:T(2,128)} %fusion.28), calls=%async_computation | async-start | bytes 1310720 | tf_op jit(solution)/shard_map/all_to_all | solution.py:103
